TPU v7x, 256 devices: a whole 4x4x8 slice. The times are simulated.
256 devices in a mesh: dp: 8 (over x_hi, y), fsdp: 16 (over z, core), tensor: 2 (over x_lo).
Axes of the slice: x: 4 (x_hi: 2, x_lo: 2; x = x_hi * 2 + x_lo), y: 4, z: 8, core: 2. Of those that a mesh axis runs over, the one named last changes fastest.
Arguments:
- attn_out: bfloat16 [16384, 2560], P(('dp', 'fsdp')), may hold values from -6 to 6
- cotangent: bfloat16 [16384, 5120], P(('dp', 'fsdp'), 'tensor'), may hold values from -6 to 6
- old_weights: bfloat16 [3, 2048, 4096], P(None, 'tensor', 'fsdp'), may hold values from -0.125 to 0.125
- depth_coef: float32 [2], replicated, may hold values from 0.3 to 1
- depth_pick: int32 [2], replicated, may hold values from 0 to 2
- in_blocks: bfloat16 [20, 2, 128, 128], replicated, may hold values from -0.3125 to 0.3125
- in_cols: int32 [20, 2], replicated, may hold values from 0 to 15, all different within a row
- out_blocks: bfloat16 [40, 2, 128, 128], P('tensor'), may hold values from -0.375 to 0.375
- out_cols: int32 [40, 2], P('tensor'), may hold values from 0 to 31, all different within a row
Outputs:
- grown_out: bfloat16 [16384, 5120], P(('dp', 'fsdp'), 'tensor')
- grad_attn: bfloat16 [16384, 2560], P(('dp', 'fsdp'), 'tensor')
- grad_in_blocks: float32 [20, 2, 128, 128], P('tensor')
- grad_out_blocks: float32 [40, 2, 128, 128], P('tensor')
Inputs may be any that keep to these rules, and one draw needn't show every extreme that they name: `in_cols`: each row names 2 different old head blocks; every old head block is named by some row. `out_cols`: each row names 2 different old width blocks; every old width block is named by some row.
All inputs are finite; a program needn't handle non-finite values.
Results may differ from a plain program's by a relative error of at most 0.0095.
Values may be sent and summed in bfloat16 or wider, within the bound.
No kernel may reach another device: no remote copies, remote signals or barrier semaphores. Data moves between devices by JAX's collectives and lax.ppermute only.
A program may use at most 64 MiB of HBM per device.

v0:
```python
import jax
import jax.numpy as jnp
from jax import lax
from jax.sharding import Mesh
from jax.sharding import PartitionSpec as P

HEAD = 128
D_OLD = 4096
HG_OLD = 16
HG_NEW = 20
DEPTH_K = 2
BO_OLD = 32
PEERS = ("xh", "y", "z")


def gathered_mix(mixed_weight):
    return lax.all_gather(mixed_weight, ("z", "c"), axis=1, tiled=True)


def pair_sum(part):
    other = lax.ppermute(part, "xl", [(0, 1), (1, 0)])
    return (part.astype(jnp.float32) + other.astype(jnp.float32)).astype(jnp.bfloat16)


def token_sum(in_terms, out_terms, scale):
    core = lax.axis_index("c")
    peers = lax.axis_size(PEERS)
    ri, ro = (in_terms.shape[0] // 2, out_terms.shape[0] // 2)

    def half(which):
        a = lax.dynamic_slice_in_dim(in_terms, which * ri, ri, 0).reshape(-1, HEAD)
        b = lax.dynamic_slice_in_dim(out_terms, which * ro, ro, 0).reshape(-1, HEAD)
        return jnp.concatenate([a, b], axis=0)

    swap = [(0, 1), (1, 0)]
    other = lax.ppermute(half(1 - core).astype(jnp.bfloat16), "c", swap)
    mine = (half(core) + other.astype(jnp.float32)).astype(jnp.bfloat16)
    rows = mine.shape[0]
    mine = mine.reshape(peers, rows // peers, HEAD)
    parts = lax.all_to_all(mine, PEERS, 0, 0, tiled=True)
    total = (jnp.sum(parts.astype(jnp.float32), axis=0) * scale).astype(jnp.bfloat16)
    spread = jnp.broadcast_to(total[None], mine.shape)
    full = lax.all_to_all(spread, PEERS, 0, 0, tiled=True).reshape(rows, HEAD)
    theirs = lax.ppermute(full, "c", swap)
    first = jnp.where(core == 0, full, theirs).astype(jnp.float32)
    second = jnp.where(core == 0, theirs, full).astype(jnp.float32)
    cut = ri * in_terms.shape[1] * HEAD
    in_sum = jnp.concatenate([first[:cut], second[:cut]], 0).reshape(in_terms.shape)
    out_sum = jnp.concatenate([first[cut:], second[cut:]], 0).reshape(out_terms.shape)
    return (in_sum, out_sum)


def local(
    attn_out,
    cotangent,
    old_weights,
    depth_coef,
    depth_pick,
    in_blocks,
    in_cols,
    out_blocks,
    out_cols,
):
    highest = lax.Precision.HIGHEST
    tok_rows = attn_out.shape[0]
    tensor_half = lax.axis_index("xl")
    tensor_count = lax.axis_size("xl")
    local_old = old_weights.shape[1]
    local_blocks = local_old // HEAD
    rows_in = HG_NEW // tensor_count
    mixed_weight = jnp.zeros(old_weights.shape[1:], jnp.float32)
    for layer_slot in range(DEPTH_K):
        picked = lax.dynamic_index_in_dim(old_weights, depth_pick[layer_slot], 0, keepdims=False)
        mixed_weight = mixed_weight + depth_coef[layer_slot] * picked.astype(jnp.float32)
    mixed_weight = mixed_weight.astype(jnp.bfloat16)
    attn_blocks = attn_out.reshape(tok_rows, HG_NEW, HEAD)
    products = jnp.einsum(
        "trd,rkde->trke", attn_blocks, in_blocks, preferred_element_type=jnp.float32
    )
    local_cols = tensor_half * local_blocks + jnp.arange(local_blocks, dtype=jnp.int32)
    in_hot = (in_cols[:, :, None] == local_cols[None, None, :]).astype(jnp.float32)
    hidden_local = jnp.einsum("trke,rkc->tce", products, in_hot, precision=highest)
    hidden_local = hidden_local.reshape(tok_rows, local_old).astype(jnp.bfloat16)
    full_mix = gathered_mix(mixed_weight)
    old_part = jnp.dot(hidden_local, full_mix, preferred_element_type=jnp.float32)
    old_out = pair_sum(old_part.astype(jnp.bfloat16))
    old_selected = jnp.take(old_out.reshape(tok_rows, BO_OLD, HEAD), out_cols, axis=1)
    grown_out = jnp.einsum(
        "trkd,rkde->tre", old_selected, out_blocks, preferred_element_type=jnp.float32
    )
    grown_out = grown_out.reshape(tok_rows, -1).astype(jnp.bfloat16)
    cot_blocks = cotangent.reshape(tok_rows, out_blocks.shape[0], HEAD)
    backward_terms = jnp.einsum(
        "tre,rkde->trkd", cot_blocks, out_blocks, preferred_element_type=jnp.float32
    )
    out_hot = (out_cols[:, :, None] == jnp.arange(BO_OLD, dtype=jnp.int32)[None, None, :]).astype(
        jnp.float32
    )
    grad_part = jnp.einsum("trkd,rkc->tcd", backward_terms, out_hot, precision=highest).reshape(
        tok_rows, D_OLD
    )
    old_grad = pair_sum(grad_part.astype(jnp.bfloat16))
    hidden_grad_local = jnp.einsum(
        "to,fo->tf", old_grad, full_mix, preferred_element_type=jnp.float32
    ).astype(jnp.bfloat16)
    hidden_grad = lax.all_gather(hidden_grad_local, "xl", axis=1, tiled=True)
    my_in_blocks = lax.dynamic_slice_in_dim(in_blocks, tensor_half * rows_in, rows_in, 0)
    my_in_cols = lax.dynamic_slice_in_dim(in_cols, tensor_half * rows_in, rows_in, 0)
    grad_selected = jnp.take(hidden_grad.reshape(tok_rows, HG_OLD, HEAD), my_in_cols, axis=1)
    grad_attn = jnp.einsum(
        "trke,rkde->trd", grad_selected, my_in_blocks, preferred_element_type=jnp.float32
    )
    grad_attn = grad_attn.reshape(tok_rows, rows_in * HEAD).astype(jnp.bfloat16)
    my_attn = lax.dynamic_slice_in_dim(attn_blocks, tensor_half * rows_in, rows_in, 1)
    in_terms = jnp.einsum(
        "trd,trke->rkde", my_attn, grad_selected, preferred_element_type=jnp.float32
    )
    out_terms = jnp.einsum(
        "trkd,tre->rkde", old_selected, cot_blocks, preferred_element_type=jnp.float32
    )
    grad_scale = float(tok_rows * lax.axis_size(PEERS) * lax.axis_size("c")) ** (-0.5)
    in_sum, out_sum = token_sum(in_terms, out_terms, grad_scale)
    return (grown_out, grad_attn, in_sum, out_sum)


def solution(mesh):
    fine = Mesh(mesh.devices.reshape(2, 4, 8, 2, 2), ("xh", "y", "z", "c", "xl"))
    tokens = ("xh", "y", "z", "c")
    placed = (
        P(tokens, None),
        P(tokens, "xl"),
        P(None, "xl", ("z", "c")),
        P(),
        P(),
        P(),
        P(),
        P("xl", None, None, None),
        P("xl", None),
    )
    return jax.shard_map(
        local,
        mesh=fine,
        in_specs=placed,
        out_specs=(
            P(tokens, "xl"),
            P(tokens, "xl"),
            P("xl", None, None, None),
            P("xl", None, None, None),
        ),
        check_vma=False,
    )
```

profile of v0, /device:TPU:1, one launch (start us, length us, event | category | flops | bytes accessed | tf_op | source)
XLA Modules:
  0.0 239.7 jit_solution(4200298776029856514)
XLA Ops:
  7.2 0.0 copy-start
  7.2 0.0 all-gather.3.cloned.1.call-start
  7.2 1.4 fusion.55
  11.2 1.3 fusion.54
  13.8 3.4 %add_convert_fusion.3 = bf16[1,1024,256]{2,1,0:T(8,128)(2,1)} fusion(bf16[3,1024,256]{2,1,0:T(8,128)(2,1)} %param.11, s32[]{:T(128)S(6)} %select_n.56, f32[]{:T(128)} %bitcast.10, s32[]{:T(128)S(6)} %select_n.55, f32[]{:T(128)} %bitcast.8), kind=kLoop, calls=%fused_computation.34 | loop fusion | flops 1572864 | bytes 1572880 | tf_op jit(solution)/shard_map/convert_element_type | solution.py:75
  17.2 0.0 all-gather.3.cloned.1.call-update
  17.3 0.3 copy.33
  17.6 2.0 fusion.57
  19.6 3.6 %copy.46 = f32[20,2,128,128]{2,0,1,3:T(8,128)} copy(f32[20,2,128,128]{3,2,1,0:T(8,128)} %fusion.57) | data formatting | bytes 5242880 | tf_op jit(solution)/shard_map/tre,rkde->trkd/dot_general | solution.py:93
  23.1 3.3 %bitcast_convert_fusion = bf16[32,128,128]{2,0,1:T(8,128)(2,1)S(1)} fusion(f32[20,2,128,128]{2,0,1,3:T(8,128)} %copy.46, s32[20,2]{0,1:T(2,128)S(1)} %copy-done.11), kind=kOutput, calls=%fused_computation.12 | convolution fusion | flops 252183808 | bytes 3670176 | tf_op jit(solution)/shard_map/trkd,rkc->tcd/dot_general | solution.py:99
  26.5 0.0 copy-start.10
  26.5 1.5 copy.67
  27.9 2.0 collective-permute-start.1
  30.0 0.1 compare_and_fusion
  30.1 0.1 copy.32
  30.2 0.1 copy.25
  30.3 0.1 copy.34
  30.4 0.1 reshape.104
  30.5 0.1 copy.27
  30.6 0.1 reshape.96
  30.7 2.2 copy.26
  32.8 3.6 %fusion.56 = f32[20,2,128,128]{3,2,1,0:T(8,128)} fusion(bf16[20,2,128,128]{3,2,1,0:T(8,128)(2,1)} %param.14, bf16[128,20,128,1]{0,2,3,1:T(8,128)(2,1)} %bitcast.130), kind=kOutput, calls=%fused_computation.79 | convolution fusion | flops 167772160 | bytes 4587520 | tf_op jit(solution)/shard_map/trd,rkde->trke/dot_general | solution.py:77
  36.4 3.6 %copy.40 = f32[20,2,128,128]{2,0,1,3:T(8,128)} copy(f32[20,2,128,128]{3,2,1,0:T(8,128)} %fusion.56) | data formatting | bytes 5242880 | tf_op jit(solution)/shard_map/trd,rkde->trke/dot_general | solution.py:77
  40.0 3.0 %fusion.22 = bf16[8,128,128]{2,0,1:T(8,128)(2,1)S(1)} fusion(f32[20,2,128,128]{2,0,1,3:T(8,128)} %copy.40, s32[20,2]{0,1:T(2,128)S(1)} %copy-done.10, s32[8]{0:T(128)S(1)} %iota_add_fusion), kind=kOutput, calls=%fused_computation.29 | convolution fusion | flops 63045952 | bytes 2883776 | tf_op jit(solution)/shard_map/trke,rkc->tce/dot_general | solution.py:82
  43.0 43.8 %all-gather.3.cloned.1.call-done = bf16[1,1024,4096]{2,1,0:T(8,128)(2,1)} async-done(((bf16[1,1024,256]{2,1,0:T(8,128)(2,1)}), bf16[1,1024,4096]{2,1,0:T(8,128)(2,1)}) %all-gather.3.cloned.1.call-update) | async-done | bytes 8388624 | tf_op jit(solution)/shard_map/all_gather | solution.py:17
  86.8 5.8 %fusion.4 = bf16[128,4096]{1,0:T(8,128)(2,1)} fusion(bf16[1,1024,4096]{2,1,0:T(8,128)(2,1)} %all-gather.3.cloned.1.call-done, bf16[16,8,8,128]{3,2,1,0:T(8,128)(2,1)S(1)} %bitcast.137), kind=kOutput, calls=%fused_computation.6 | convolution fusion | flops 1074266112 | bytes 9699328 | tf_op jit(solution)/shard_map/dot_general | solution.py:85
  92.6 0.0 collective-permute-start
  92.6 4.1 %fusion.25 = bf16[128,1024]{1,0:T(8,128)(2,1)S(1)} fusion(bf16[1,1024,4096]{2,1,0:T(8,128)(2,1)S(1)} %copy-done.1, bf16[128,4096]{1,0:T(8,128)(2,1)} %collective-permute-done.1, bf16[16,8,32,128]{3,2,1,0:T(8,128)(2,1)S(1)} %bitcast.125), kind=kOutput, calls=%fused_computation.30 | convolution fusion | flops 1075970048 | bytes 10747904 | tf_op jit(solution)/shard_map/to,fo->tf/dot_general | solution.py:103
  96.8 0.0 copy-start.4
  96.8 26.1 %all_gather.7 = bf16[128,2048]{1,0:T(8,128)(2,1)S(1)} all-gather(bf16[128,1024]{1,0:T(8,128)(2,1)S(1)} %fusion.25), channel_id=1, replica_groups=mesh['xh'=2,'y'=4,'z'=8,'c'=2,'xl'=2] {'xl'}, dimensions={1}, use_global_device_ids=true | all-gather | bytes 786432 | tf_op jit(solution)/shard_map/all_gather | solution.py:106
  122.9 0.1 copy_bitcast_fusion.2
  123.0 1.5 gather_fusion.1
  124.5 1.5 fusion.29
  126.0 0.1 dynamic-slice_convert_fusion.1
  126.1 1.0 copy-done.5
  127.1 1.9 copy_bitcast_fusion.1
  129.0 1.8 gather_fusion
  130.8 2.4 %copy.29 = bf16[20,2,128,128]{2,3,1,0:T(8,128)(2,1)} copy(bf16[20,2,128,128]{3,2,1,0:T(8,128)(2,1)} %bitcast.128) | data formatting | bytes 2621440 | tf_op jit(solution)/shard_map/jit(_take)/gather | solution.py:87
  133.2 1.9 fusion.15
  135.1 0.0 copy-start.2
  135.1 1.5 copy-done.2
  136.6 0.1 dynamic-slice_convert_fusion
  136.7 1.0 pad_maximum_fusion.2
  137.7 1.1 collective-permute-start.2
  138.9 1.4 constant_dynamic-slice_fusion
  140.3 1.1 collective-permute-done.2
  141.4 1.4 fusion.11
  142.8 0.2 reshape.90
  143.0 38.0 %all_to_all.10 = bf16[64,60,128]{2,1,0:T(8,128)(2,1)S(1)} all-to-all(bf16[64,60,128]{2,1,0:T(8,128)(2,1)S(1)} %reshape.90), channel_id=1, replica_groups=mesh['xh'=2,'y'=4,'z'=8,'c'=2,'xl'=2] {'xh','y','z'}, dimensions={0} | all-to-all | bytes 1966080 | tf_op jit(solution)/shard_map/all_to_all | solution.py:40
  180.9 0.2 convert_reduce_fusion
  181.1 0.2 broadcast_in_dim.40
  181.4 34.7 %all_to_all.11 = bf16[64,60,128]{2,1,0:T(8,128)(2,1)} all-to-all(bf16[64,60,128]{2,1,0:T(8,128)(2,1)S(1)} %broadcast_in_dim.40), channel_id=1, replica_groups=mesh['xh'=2,'y'=4,'z'=8,'c'=2,'xl'=2] {'xh','y','z'}, dimensions={0} | all-to-all | bytes 1966080 | tf_op jit(solution)/shard_map/all_to_all | solution.py:43
  216.2 2.2 reshape.91
  218.4 4.0 %collective-permute-start.3 = (bf16[3840,128]{1,0:T(8,128)(2,1)}, bf16[3840,128]{1,0:T(8,128)(2,1)}, u32[]{:S(2)}, u32[]{:S(2)}) collective-permute-start(bf16[3840,128]{1,0:T(8,128)(2,1)} %reshape.91), channel_id=1, source_target_pairs={{0,2},{2,0},{1,3},{3,1},{4,6},{6,4},{5,7},{7,5},{8,10},{10,8},{9,1... | collective-permute-start | bytes 2949128 | tf_op jit(solution)/shard_map/ppermute | solution.py:44
  222.3 2.2 fusion.21
  224.6 1.9 copy.38
  226.4 0.6 fusion.14
  227.1 1.1 copy.37
  228.2 0.2 copy-done.7
  228.3 1.5 select_convert_fusion.1
  229.8 0.1 slice.38
  230.0 0.1 slice.39
  230.1 1.7 pad_maximum_fusion
  231.7 1.1 pad_maximum_fusion.1
  (29 shorter events, 0.2 us)
Async XLA Ops:
  7.2 10.4 %copy-start = (bf16[20,2,128,128]{3,2,1,0:T(8,128)(2,1)S(1)}, bf16[20,2,128,128]{3,2,1,0:T(8,128)(2,1)}, u32[]{:S(2)}) copy-start(bf16[20,2,128,128]{3,2,1,0:T(8,128)(2,1)} %param.16) | copy-start | bytes 3932164
  7.2 10.1 %copy-start.9 = (bf16[128,2560]{1,0:T(8,128)(2,1)S(1)}, bf16[128,2560]{1,0:T(8,128)(2,1)}, u32[]{:S(2)}) copy-start(bf16[128,2560]{1,0:T(8,128)(2,1)} %param.10) | copy-start | bytes 1966084
  7.2 79.6 %all-gather.3.cloned.1.call-start = ((), (), s32[]{:S(2)}) async-start(), calls=%async_computation.2 | async-start | bytes 8912896 | tf_op jit(solution)/shard_map/all_gather | solution.py:17
  19.6 3.6 %copy-start.11 = (s32[20,2]{0,1:T(2,128)S(1)}, s32[20,2]{0,1:T(2,128)}, u32[]{:S(2)}) copy-start(s32[20,2]{0,1:T(2,128)} %param.17) | copy-start | bytes 484
  26.5 3.5 %copy-start.10 = (s32[20,2]{0,1:T(2,128)S(1)}, s32[20,2]{0,1:T(2,128)}, u32[]{:S(2)}) copy-start(s32[20,2]{0,1:T(2,128)} %param.15) | copy-start | bytes 484
  27.9 64.7 %collective-permute-start.1 = (bf16[128,4096]{1,0:T(8,128)(2,1)}, bf16[128,4096]{1,0:T(8,128)(2,1)}, u32[]{:S(2)}, u32[]{:S(2)}) collective-permute-start(bf16[128,4096]{1,0:T(8,128)(2,1)} %bitcast.123), channel_id=1, source_target_pairs={{0,1},{1,0},{2,3},{3,2},{4,5},{5,4},{6,7},{7,6},{8,9},{9,8},{10,11... | collective-permute-start | bytes 3145736 | tf_op jit(solution)/shard_map/ppermute | solution.py:21
  86.8 5.8 %copy-start.1 = (bf16[1,1024,4096]{2,1,0:T(8,128)(2,1)S(1)}, bf16[1,1024,4096]{2,1,0:T(8,128)(2,1)}, u32[]{:S(2)}) copy-start(bf16[1,1024,4096]{2,1,0:T(8,128)(2,1)} %all-gather.3.cloned.1.call-done) | copy-start | bytes 25165828
  92.6 34.5 %collective-permute-start = (bf16[128,4096]{1,0:T(8,128)(2,1)}, bf16[128,4096]{1,0:T(8,128)(2,1)}, u32[]{:S(2)}, u32[]{:S(2)}) collective-permute-start(bf16[128,4096]{1,0:T(8,128)(2,1)} %fusion.4), channel_id=1, source_target_pairs={{0,1},{1,0},{2,3},{3,2},{4,5},{5,4},{6,7},{7,6},{8,9},{9,8},{10,11... | collective-permute-start | bytes 3145736 | tf_op jit(solution)/shard_map/ppermute | solution.py:21
  96.8 27.8 %copy-start.4 = (bf16[128,2560]{0,1:T(8,128)(2,1)S(1)}, bf16[128,2560]{0,1:T(8,128)(2,1)}, u32[]{:S(2)}) copy-start(bf16[128,2560]{0,1:T(8,128)(2,1)} %copy.26) | copy-start | bytes 1966084
  126.0 1.1 copy-start.5
  135.1 1.5 copy-start.2
  136.6 2.2 copy-start.6
  137.7 3.7 %collective-permute-start.2 = (bf16[3840,128]{1,0:T(8,128)(2,1)}, bf16[3840,128]{1,0:T(8,128)(2,1)}, u32[]{:S(2)}, u32[]{:S(2)}) collective-permute-start(bf16[3840,128]{1,0:T(8,128)(2,1)} %pad_maximum_fusion.2), channel_id=1, source_target_pairs={{0,2},{2,0},{1,3},{3,1},{4,6},{6,4},{5,7},{7,5},{8,10},{10,8},{9,1... | collective-permute-start | bytes 2949128 | tf_op jit(solution)/shard_map/ppermute | solution.py:36
  181.4 40.9 %copy-start.8 = (bf16[20,128,128]{2,1,0:T(8,128)(2,1)S(1)}, bf16[20,128,128]{2,1,0:T(8,128)(2,1)}, u32[]{:S(2)}) copy-start(bf16[20,128,128]{2,1,0:T(8,128)(2,1)} %gather_fusion.1) | copy-start | bytes 1966084
  216.2 10.3 %copy-start.3 = (bf16[20,2,128,128]{2,3,1,0:T(8,128)(2,1)S(1)}, bf16[20,2,128,128]{2,3,1,0:T(8,128)(2,1)}, u32[]{:S(2)}) copy-start(bf16[20,2,128,128]{2,3,1,0:T(8,128)(2,1)} %copy.29) | copy-start | bytes 3932164
  218.4 9.8 %collective-permute-start.3 = (bf16[3840,128]{1,0:T(8,128)(2,1)}, bf16[3840,128]{1,0:T(8,128)(2,1)}, u32[]{:S(2)}, u32[]{:S(2)}) collective-permute-start(bf16[3840,128]{1,0:T(8,128)(2,1)} %reshape.91), channel_id=1, source_target_pairs={{0,2},{2,0},{1,3},{3,1},{4,6},{6,4},{5,7},{7,5},{8,10},{10,8},{9,1... | collective-permute-start | bytes 2949128 | tf_op jit(solution)/shard_map/ppermute | solution.py:44
  227.1 1.3 copy-start.7
Sparse Core Ops, SparseCore 0:
  17.4 69.4 all-gather.2
where the time goes:
time: 241 us; the launch traced here: 240 us
  blocking collectives  98.8 us (41%)
  waiting for transfers between devices  44.9 us (19%)
  local copies, waits for them, and re-layouts  30.4 us (13%)
  matrix products  28 us (12%)
  between operations  18.2 us (8%)
  other arithmetic  12.2 us (5%)
  starting transfers between devices  7.18 us (3%)
    all_gather x1, waiting for transfers between devices, gathered_mix(): return lax.all_gather(mixed_weight, ('z', 'c'), axis=1, tiled=True)  43.8 us
    all_to_all x1, blocking collectives, token_sum(): parts = lax.all_to_all(mine, PEERS, 0, 0, tiled=True)  38 us
    all_to_all x1, blocking collectives, token_sum(): full = lax.all_to_all(spread, PEERS, 0, 0, tiled=True).reshape(rows, HEAD)  34.7 us
    all_gather x1, blocking collectives, local(): hidden_grad = lax.all_gather(hidden_grad_local, 'xl', axis=1, tiled=True)  26.1 us
    unnamed x29, local copies, waits for them, and re-layouts  9.58 us
    dot_general x1, matrix products, local(): jnp.dot(hidden_local, full_mix, preferred_element_type=jnp.float32)  5.77 us
  transfers between devices with their start and end apart: 5, of which 2 were waited for; matrix products, arithmetic and copies ran while one was open for 18% of the time, Pallas kernels for 0%

commit v1 on v0

--- a/solution.py
+++ b/solution.py
@@ -14,7 +14,10 @@
 
 
 def gathered_mix(mixed_weight):
-    return lax.all_gather(mixed_weight, ("z", "c"), axis=1, tiled=True)
+    return jnp.concatenate(
+        lax.all_to_all(jnp.stack([mixed_weight] * lax.axis_size(("z", "c"))), ("z", "c"), 0, 0),
+        axis=1,
+    )
 
 
 def pair_sum(part):

time: 241 us -> 357 us (1.48)
  waiting for transfers between devices: 44.9 us -> 160 us
  between operations: 18.2 us -> 4.8 us
  starting transfers between devices: 7.18 us -> 18.3 us
  local copies, waits for them, and re-layouts: 30.4 us -> 34.8 us
    all_to_all x0 -> x1, waiting for transfers between devices: none -> 159 us  [gathered_mix(): lax.all_to_all(jnp.stack([mixed_weight] * lax.axis_size(('z', 'c'))), ('z...]
    all_gather x1 -> x0, waiting for transfers between devices: 43.8 us -> none  [gathered_mix(): return lax.all_gather(mixed_weight, ('z', 'c'), axis=1, tiled=True)]
    all_to_all x0 -> x1, starting transfers between devices: none -> 10.1 us  [gathered_mix(): lax.all_to_all(jnp.stack([mixed_weight] * lax.axis_size(('z', 'c'))), ('z...]
    another operation x3 -> x5, local copies, waits for them, and re-layouts: 0.21 us -> 4.73 us  [the longest x2 4.52 us: gathered_mix(): jnp.stack([mixed_weight] * lax.axis_size(('z', 'c')))]
    unnamed x29 -> x27, local copies, waits for them, and re-layouts: 9.58 us -> 9.54 us
  transfers between devices with their start and end apart: 5 -> 5, of which waited for: 2 -> 2; matrix products, arithmetic and copies ran while one was open for 18% -> 13% of each run, Pallas kernels for 0% -> 0%
where the time goes in v1:
time: 357 us; the launch traced here: 356 us
  waiting for transfers between devices  160 us (45%)
  blocking collectives  96.6 us (27%)
  local copies, waits for them, and re-layouts  34.8 us (10%)
  matrix products  30.6 us (9%)
  starting transfers between devices  18.3 us (5%)
  other arithmetic  11.5 us (3%)
  between operations  4.8 us (1%)
    all_to_all x1, waiting for transfers between devices, gathered_mix(): lax.all_to_all(jnp.stack([mixed_weight] * lax.axis_size(('z', 'c'))), ('z...  159 us
    all_to_all x1, blocking collectives, token_sum(): parts = lax.all_to_all(mine, PEERS, 0, 0, tiled=True)  38.8 us
    all_to_all x1, blocking collectives, token_sum(): full = lax.all_to_all(spread, PEERS, 0, 0, tiled=True).reshape(rows, HEAD)  34.7 us
    all_gather x1, blocking collectives, local(): hidden_grad = lax.all_gather(hidden_grad_local, 'xl', axis=1, tiled=True)  23.1 us
    all_to_all x1, starting transfers between devices, gathered_mix(): lax.all_to_all(jnp.stack([mixed_weight] * lax.axis_size(('z', 'c'))), ('z...  10.1 us
    unnamed x27, local copies, waits for them, and re-layouts  9.54 us
    dot_general x1, matrix products, local(): jnp.dot(hidden_local, full_mix, preferred_element_type=jnp.float32)  7.25 us
  transfers between devices with their start and end apart: 5, of which 2 were waited for; matrix products, arithmetic and copies ran while one was open for 13% of the time, Pallas kernels for 0%

profile of v1, /device:TPU:1, one launch (start us, length us, event | category | flops | bytes accessed | tf_op | source)
XLA Modules:
  0.0 356.3 jit_solution(8879445128310491203)
XLA Ops:
  0.6 0.0 copy-start
  0.6 1.4 fusion.46
  4.6 1.3 fusion.45
  7.2 2.7 fusion.25
  9.9 0.2 copy.27
  10.1 4.3 %stack.5 = bf16[16,1024,256]{1,2,0:T(8,128)(2,1)} broadcast(bf16[1024,256]{0,1:T(8,128)(2,1)S(1)} %copy.27), dimensions={1,2} | broadcast | bytes 8912896 | tf_op jit(solution)/shard_map/stack | solution.py:18
  14.4 10.1 %all-to-all-start = ((bf16[16,1024,256]{1,2,0:T(8,128)(2,1)}), bf16[16,1024,256]{1,2,0:T(8,128)(2,1)}, u32[]{:S(2)}, u32[]{:S(2)}) async-start(bf16[16,1024,256]{1,2,0:T(8,128)(2,1)} %stack.5), calls=%async_computation | async-start | bytes 16777216 | tf_op jit(solution)/shard_map/all_to_all | solution.py:18
  24.5 0.3 copy.34
  24.9 2.0 fusion.48
  26.9 3.5 copy.47
  30.4 3.3 bitcast_convert_fusion
  33.7 0.0 copy-start.9
  33.7 1.4 copy.68
  35.2 1.2 collective-permute-start.1
  36.4 0.1 compare_and_fusion
  36.4 0.1 copy.35
  36.5 0.1 reshape.105
  36.6 0.1 copy.33
  36.7 2.2 copy.26
  38.9 3.5 fusion.47
  42.4 3.5 copy.41
  45.9 0.1 copy.28
  46.0 0.1 reshape.97
  46.2 0.1 copy.25
  46.3 3.0 fusion.15
  49.3 158.6 %all-to-all-done = bf16[16,1024,256]{1,2,0:T(8,128)(2,1)} async-done(((bf16[16,1024,256]{1,2,0:T(8,128)(2,1)}), bf16[16,1024,256]{1,2,0:T(8,128)(2,1)}, u32[]{:S(2)}, u32[]{:S(2)}) %all-to-all-start) | async-done | bytes 8388640 | tf_op jit(solution)/shard_map/all_to_all | solution.py:18
  207.9 7.2 %convolution_convert_fusion = bf16[128,4096]{1,0:T(8,128)(2,1)} fusion(bf16[1024,4096]{0,1:T(8,128)(2,1)} %bitcast.14, bf16[16,8,8,128]{3,2,1,0:T(8,128)(2,1)S(1)} %bitcast.137), kind=kOutput, calls=%fused_computation.2 | convolution fusion | flops 1074266112 | bytes 9699328 | tf_op jit(solution)/shard_map/dot_general | solution.py:88
  215.2 1.2 collective-permute-start
  216.4 5.3 %convolution_convert_fusion.1 = bf16[128,1024]{1,0:T(8,128)(2,1)S(1)} fusion(bf16[1024,4096]{0,1:T(8,128)(2,1)} %bitcast.14, bf16[128,4096]{1,0:T(8,128)(2,1)} %collective-permute-done.1, bf16[16,8,32,128]{3,2,1,0:T(8,128)(2,1)S(1)} %bitcast.123), kind=kOutput, calls=%fused_computation.26 | convolution fusion | flops 1075970048 | bytes 10747904 | tf_op jit(solution)/shard_map/to,fo->tf/dot_general | solution.py:106
  221.7 0.0 copy-start.3
  221.7 23.1 %all_gather.3 = bf16[128,2048]{1,0:T(8,128)(2,1)S(1)} all-gather(bf16[128,1024]{1,0:T(8,128)(2,1)S(1)} %convolution_convert_fusion.1), channel_id=1, replica_groups=mesh['xh'=2,'y'=4,'z'=8,'c'=2,'xl'=2] {'xl'}, dimensions={1}, use_global_device_ids=true | all-gather | bytes 786432 | tf_op jit(solution)/shard_map/all_gather | solution.py:109
  244.7 0.1 copy_bitcast_fusion.2
  244.9 1.5 gather_fusion.1
  246.4 1.5 fusion.19
  247.9 0.1 dynamic-slice_convert_fusion.1
  248.0 1.0 copy-done.4
  249.0 1.9 copy_bitcast_fusion.1
  250.8 1.8 gather_fusion
  252.7 2.4 copy.30
  255.1 1.9 fusion.8
  257.0 1.5 copy-done.1
  258.5 0.1 dynamic-slice_convert_fusion
  258.6 1.0 pad_maximum_fusion.2
  259.6 1.8 collective-permute-start.2
  261.5 1.4 constant_dynamic-slice_fusion
  262.9 1.1 collective-permute-done.2
  264.0 1.4 fusion.4
  265.4 0.2 reshape.91
  265.6 38.8 %all_to_all.15 = bf16[64,60,128]{2,1,0:T(8,128)(2,1)S(1)} all-to-all(bf16[64,60,128]{2,1,0:T(8,128)(2,1)S(1)} %reshape.91), channel_id=1, replica_groups=mesh['xh'=2,'y'=4,'z'=8,'c'=2,'xl'=2] {'xh','y','z'}, dimensions={0} | all-to-all | bytes 1966080 | tf_op jit(solution)/shard_map/all_to_all | solution.py:43
  304.3 0.2 convert_reduce_fusion
  304.5 0.2 broadcast_in_dim.40
  304.8 34.7 %all_to_all.16 = bf16[64,60,128]{2,1,0:T(8,128)(2,1)} all-to-all(bf16[64,60,128]{2,1,0:T(8,128)(2,1)S(1)} %broadcast_in_dim.40), channel_id=1, replica_groups=mesh['xh'=2,'y'=4,'z'=8,'c'=2,'xl'=2] {'xh','y','z'}, dimensions={0} | all-to-all | bytes 1966080 | tf_op jit(solution)/shard_map/all_to_all | solution.py:46
  339.5 2.2 reshape.92
  341.7 4.0 %collective-permute-start.3 = (bf16[3840,128]{1,0:T(8,128)(2,1)}, bf16[3840,128]{1,0:T(8,128)(2,1)}, u32[]{:S(2)}, u32[]{:S(2)}) collective-permute-start(bf16[3840,128]{1,0:T(8,128)(2,1)} %reshape.92), channel_id=1, source_target_pairs={{0,2},{2,0},{1,3},{3,1},{4,6},{6,4},{5,7},{7,5},{8,10},{10,8},{9,1... | collective-permute-start | bytes 2949128 | tf_op jit(solution)/shard_map/ppermute | solution.py:47
  345.7 2.2 fusion.14
  347.9 1.9 copy.39
  349.8 0.6 fusion.7
  350.5 1.1 copy.38
  351.5 0.2 copy-done.6
  351.7 1.5 select_convert_fusion.1
  353.2 0.1 slice.38
  353.3 0.1 slice.39
  353.5 1.7 pad_maximum_fusion
  355.1 1.1 pad_maximum_fusion.1
  (28 shorter events, 0.2 us)
Async XLA Ops:
  0.6 24.2 %copy-start = (bf16[20,2,128,128]{3,2,1,0:T(8,128)(2,1)S(1)}, bf16[20,2,128,128]{3,2,1,0:T(8,128)(2,1)}, u32[]{:S(2)}) copy-start(bf16[20,2,128,128]{3,2,1,0:T(8,128)(2,1)} %param.16) | copy-start | bytes 3932164
  14.4 10.1 %copy-start.8 = (bf16[128,2560]{1,0:T(8,128)(2,1)S(1)}, bf16[128,2560]{1,0:T(8,128)(2,1)}, u32[]{:S(2)}) copy-start(bf16[128,2560]{1,0:T(8,128)(2,1)} %param.10) | copy-start | bytes 1966084
  14.4 193.5 %all-to-all-start = ((bf16[16,1024,256]{1,2,0:T(8,128)(2,1)}), bf16[16,1024,256]{1,2,0:T(8,128)(2,1)}, u32[]{:S(2)}, u32[]{:S(2)}) async-start(bf16[16,1024,256]{1,2,0:T(8,128)(2,1)} %stack.5), calls=%async_computation | async-start | bytes 16777216 | tf_op jit(solution)/shard_map/all_to_all | solution.py:18
  26.9 3.5 copy-start.10
  33.7 2.6 copy-start.9
  35.2 181.2 %collective-permute-start.1 = (bf16[128,4096]{1,0:T(8,128)(2,1)}, bf16[128,4096]{1,0:T(8,128)(2,1)}, u32[]{:S(2)}, u32[]{:S(2)}) collective-permute-start(bf16[128,4096]{1,0:T(8,128)(2,1)} %bitcast.121), channel_id=1, source_target_pairs={{0,1},{1,0},{2,3},{3,2},{4,5},{5,4},{6,7},{7,6},{8,9},{9,8},{10,11... | collective-permute-start | bytes 3145736 | tf_op jit(solution)/shard_map/ppermute | solution.py:24
  215.2 33.8 %collective-permute-start = (bf16[128,4096]{1,0:T(8,128)(2,1)}, bf16[128,4096]{1,0:T(8,128)(2,1)}, u32[]{:S(2)}, u32[]{:S(2)}) collective-permute-start(bf16[128,4096]{1,0:T(8,128)(2,1)} %convolution_convert_fusion), channel_id=1, source_target_pairs={{0,1},{1,0},{2,3},{3,2},{4,5},{5,4},{6,7},{7,6},{8,9},{9,8},{10,11... | collective-permute-start | bytes 3145736 | tf_op jit(solution)/shard_map/ppermute | solution.py:24
  221.7 24.7 %copy-start.3 = (bf16[128,2560]{0,1:T(8,128)(2,1)S(1)}, bf16[128,2560]{0,1:T(8,128)(2,1)}, u32[]{:S(2)}) copy-start(bf16[128,2560]{0,1:T(8,128)(2,1)} %copy.26) | copy-start | bytes 1966084
  247.9 1.1 copy-start.4
  257.0 1.5 copy-start.1
  258.5 3.0 copy-start.5
  259.6 4.4 %collective-permute-start.2 = (bf16[3840,128]{1,0:T(8,128)(2,1)}, bf16[3840,128]{1,0:T(8,128)(2,1)}, u32[]{:S(2)}, u32[]{:S(2)}) collective-permute-start(bf16[3840,128]{1,0:T(8,128)(2,1)} %pad_maximum_fusion.2), channel_id=1, source_target_pairs={{0,2},{2,0},{1,3},{3,1},{4,6},{6,4},{5,7},{7,5},{8,10},{10,8},{9,1... | collective-permute-start | bytes 2949128 | tf_op jit(solution)/shard_map/ppermute | solution.py:39
  304.8 40.9 %copy-start.7 = (bf16[20,128,128]{2,1,0:T(8,128)(2,1)S(1)}, bf16[20,128,128]{2,1,0:T(8,128)(2,1)}, u32[]{:S(2)}) copy-start(bf16[20,128,128]{2,1,0:T(8,128)(2,1)} %gather_fusion.1) | copy-start | bytes 1966084
  339.5 10.3 %copy-start.2 = (bf16[20,2,128,128]{2,3,1,0:T(8,128)(2,1)S(1)}, bf16[20,2,128,128]{2,3,1,0:T(8,128)(2,1)}, u32[]{:S(2)}) copy-start(bf16[20,2,128,128]{2,3,1,0:T(8,128)(2,1)} %copy.30) | copy-start | bytes 3932164
  341.7 9.8 %collective-permute-start.3 = (bf16[3840,128]{1,0:T(8,128)(2,1)}, bf16[3840,128]{1,0:T(8,128)(2,1)}, u32[]{:S(2)}, u32[]{:S(2)}) collective-permute-start(bf16[3840,128]{1,0:T(8,128)(2,1)} %reshape.92), channel_id=1, source_target_pairs={{0,2},{2,0},{1,3},{3,1},{4,6},{6,4},{5,7},{7,5},{8,10},{10,8},{9,1... | collective-permute-start | bytes 2949128 | tf_op jit(solution)/shard_map/ppermute | solution.py:47
  350.4 1.3 copy-start.6
